TPU v7x, 32 devices: a whole 2x2x4 slice. The times are simulated.
32 devices in a mesh: dp: 4 (over z), feat: 8 (over y, x, core).
Axes of the slice: x: 2, y: 2, z: 4, core: 2. Of those that a mesh axis runs over, the one named last changes fastest.
Arguments:
- clip_feats: bfloat16 [2, 384, 8192], P(None, 'dp', 'feat'), may hold values from 0 to 60
- proj_weight: bfloat16 [8192, 8192], P('dp', 'feat'), may hold values from -0.0625 to 0.0625
Outputs:
- loss_value: float32 [], replicated
- weight_grad: float32 [8192, 8192], P('dp', 'feat')
- redundancy: float32 [], replicated
- pair_similarity: float32 [384, 384], P('dp')
All inputs are finite; a program needn't handle non-finite values.
Results may differ from a plain program's by a relative error of at most 0.034.
Values may be sent and summed in bfloat16 or wider, within the bound.
A program may use at most 64 MiB of HBM per device.

v0:
```python
import math
import jax
import jax.numpy as jnp
from jax import lax
from jax.sharding import PartitionSpec as P

D = 8192
off_weight = 0.0051
epsilon = 1e-05
grad_scale = 32.0


def per_device(clip_feats, proj_weight):
    pairs = clip_feats.shape[1]
    width = clip_feats.shape[2]
    dp_count = lax.axis_size("dp")
    pair_count = float(pairs * dp_count)
    gathered = lax.all_gather(clip_feats, "feat", axis=2, tiled=True)
    stacked = gathered.reshape(2 * pairs, gathered.shape[2])
    projected = jnp.dot(
        stacked,
        lax.all_gather(proj_weight, "dp", axis=0, tiled=True),
        preferred_element_type=jnp.float32,
    ).reshape(2, pairs, width)
    col_mean = lax.psum(jnp.sum(projected, axis=1), "dp")[:, None, :] / pair_count
    centered = projected - col_mean
    col_var = lax.psum(jnp.sum(centered * centered, axis=1), "dp")[:, None, :] / pair_count
    col_scale = lax.rsqrt(col_var + epsilon)
    normed = centered * col_scale
    quantized = normed.astype(jnp.bfloat16)
    widened = quantized.astype(jnp.float32)
    batch_all = lax.all_gather(quantized, "dp", axis=1, tiled=True)
    gram_part = jnp.einsum("vpc,vnc->vpn", quantized, batch_all, preferred_element_type=jnp.float32)
    grams = lax.psum(gram_part, "feat")
    total_pairs = grams.shape[2]
    row_ids = (
        lax.broadcasted_iota(jnp.int32, (pairs, total_pairs), 0) + lax.axis_index("dp") * pairs
    )
    col_ids = lax.broadcasted_iota(jnp.int32, (pairs, total_pairs), 1)
    pair_similarity = jnp.where(
        row_ids == col_ids, 0.0, (grams[0] + grams[1]) / (2.0 * math.sqrt(float(D)))
    )
    diag_corr = lax.psum(jnp.sum(widened[0] * widened[1], axis=0), "dp") / pair_count
    frobenius = jnp.sum(grams[0] * grams[1])
    diag_term = jnp.sum((1.0 - diag_corr) ** 2 - off_weight * diag_corr * diag_corr)
    dp_first = (lax.axis_index("dp") == 0).astype(jnp.float32)
    feat_first = (lax.axis_index("feat") == 0).astype(jnp.float32)
    frob_scaled = feat_first * frobenius / (pair_count * pair_count)
    loss_term = dp_first * diag_term + off_weight * frob_scaled
    off_term = frob_scaled - dp_first * jnp.sum(diag_corr * diag_corr)
    total_loss, off_sum = lax.psum((loss_term, off_term), ("dp", "feat"))
    loss_value = 16.0 * total_loss / float(D)
    redundancy = 8.0 * pair_count * off_sum / (float(D) * float(D))
    slope = -2.0 * (1.0 - diag_corr) - 2.0 * off_weight * diag_corr
    coefficient = 2.0 * off_weight / (pair_count * pair_count)
    gram_q = grams.astype(jnp.bfloat16)
    cross_first = jnp.dot(gram_q[1], batch_all[0], preferred_element_type=jnp.float32)
    cross_second = jnp.dot(gram_q[0], batch_all[1], preferred_element_type=jnp.float32)
    grad_norm = jnp.stack(
        [
            slope * widened[1] / pair_count + coefficient * cross_first,
            slope * widened[0] / pair_count + coefficient * cross_second,
        ]
    )
    sum_one, sum_two = lax.psum(
        (jnp.sum(grad_norm, axis=1), jnp.sum(grad_norm * normed, axis=1)), "dp"
    )
    pre_grad = col_scale * (
        grad_norm - sum_one[:, None, :] / pair_count - normed * (sum_two[:, None, :] / pair_count)
    )
    pre_q = pre_grad.astype(jnp.bfloat16)
    flat_grad = pre_q.reshape(2 * pairs, width)
    summed = lax.psum_scatter(
        jnp.dot(stacked.T, flat_grad, preferred_element_type=jnp.float32).astype(jnp.bfloat16),
        "dp",
        scatter_dimension=0,
        tiled=True,
    ).astype(jnp.float32)
    return (loss_value, grad_scale * summed, redundancy, pair_similarity)


def solution(mesh):
    placed = (P(None, "dp", "feat"), P("dp", "feat"))
    return jax.shard_map(
        per_device,
        mesh=mesh,
        in_specs=placed,
        out_specs=(P(), P("dp", "feat"), P(), P("dp", None)),
        check_vma=False,
    )
```

profile of v0, /device:TPU:0, one launch (start us, length us, event | category | flops | bytes accessed | tf_op | source)
XLA Modules:
  0.0 791.4 jit_solution(3627898898711487195)
XLA Ops:
  7.2 0.7 all-gather.4.cloned.1.call-update
  7.9 0.7 all-gather.6.cloned.1.call-update
  8.7 36.3 %all-gather.4.cloned.1.call-done = bf16[2,96,8192]{2,1,0:T(8,128)(2,1)} async-done(((bf16[2,96,1024]{2,1,0:T(8,128)(2,1)}), bf16[2,96,8192]{2,1,0:T(8,128)(2,1)}) %all-gather.4.cloned.1.call-update) | async-done | bytes 3145744 | tf_op jit(solution)/shard_map/all_gather | solution.py:18
  45.0 288.4 %all-gather.6.cloned.1.call-done = bf16[8192,1024]{1,0:T(8,128)(2,1)} async-done(((bf16[2048,1024]{1,0:T(8,128)(2,1)}), bf16[8192,1024]{1,0:T(8,128)(2,1)}) %all-gather.6.cloned.1.call-update) | async-done | bytes 16777232 | tf_op jit(solution)/shard_map/all_gather | solution.py:22
  333.3 8.5 %fusion.16 = (f32[2,1024]{1,0:T(2,128)S(1)}, f32[2,96,1024]{2,1,0:T(8,128)S(1)}) fusion(bf16[2,96,8192]{2,1,0:T(8,128)(2,1)} %all-gather.4.cloned.1.call-done, bf16[8192,1024]{1,0:T(8,128)(2,1)} %all-gather.6.cloned.1.call-done), kind=kOutput, calls=%fused_computation.42 | convolution fusion | flops 3221420032 | bytes 20717568 | tf_op jit(solution)/shard_map/dot_general | solution.py:20
  341.8 8.8 %psum.56 = f32[2,1024]{1,0:T(2,128)S(1)} all-reduce(f32[2,1024]{1,0:T(2,128)S(1)} %get-tuple-element.19), channel_id=1, replica_groups=mesh['dp'=4,'feat'=8] {'dp'}, use_global_device_ids=true, to_apply=%region_1.0 | all-reduce | flops 2048 | bytes 16384 | tf_op jit(solution)/shard_map/psum | solution.py:25
  350.7 10.3 %psum.57 = f32[2,1024]{1,0:T(2,128)S(1)} all-reduce(f32[2,1024]{1,0:T(2,128)S(1)} %multiply_reduce_fusion.1), channel_id=1, replica_groups=mesh['dp'=4,'feat'=8] {'dp'}, use_global_device_ids=true, to_apply=%region_3.0 | all-reduce | flops 2048 | bytes 16384 | tf_op jit(solution)/shard_map/psum | solution.py:27
  361.1 0.9 fusion.14
  362.1 8.7 %psum.58 = f32[1024]{0:T(1024)S(1)} all-reduce(f32[1024]{0:T(1024)S(1)} %multiply_reduce_fusion.2), channel_id=1, replica_groups=mesh['dp'=4,'feat'=8] {'dp'}, use_global_device_ids=true, to_apply=%region_5.6 | all-reduce | flops 1024 | bytes 8192 | tf_op jit(solution)/shard_map/psum | solution.py:43
  370.8 26.6 %all-gather.8.cloned.1.call-done = bf16[2,384,1024]{2,1,0:T(8,128)(2,1)} async-done(((bf16[2,96,1024]{2,1,0:T(8,128)(2,1)}), bf16[2,384,1024]{2,1,0:T(8,128)(2,1)}) %all-gather.8.cloned.1.call-update) | async-done | bytes 1572880 | tf_op jit(solution)/shard_map/all_gather | solution.py:32
  397.3 3.0 fusion.17
  400.4 1.2 multiply_reduce_fusion.4
  401.6 50.8 %all-reduce.4.cloned.1.call-done = f32[2,96,384]{2,1,0:T(8,128)} async-done(((f32[2,96,384]{2,1,0:T(8,128)}), f32[2,96,384]{2,1,0:T(8,128)}) %all-reduce.4.cloned.1.call-update) | async-done | bytes 294928 | tf_op jit(solution)/shard_map/psum | solution.py:34
  452.4 1.0 convert_element_type.25
  453.4 1.4 fusion.4
  454.8 1.0 fusion.6
  455.8 0.7 copy-done.1
  456.8 18.7 %all-reduce.1 = (f32[2,1024]{1,0:T(2,128)S(1)}, f32[2,1024]{1,0:T(2,128)S(1)}) all-reduce(f32[2,1024]{1,0:T(2,128)S(1)} %get-tuple-element.9, f32[2,1024]{1,0:T(2,128)S(1)} %get-tuple-element.8), channel_id=1, replica_groups=mesh['dp'=4,'feat'=8] {'dp'}, use_global_device_ids=true, to_apply=%region_13.14 | all-reduce | flops 4096 | bytes 32768 | tf_op jit(solution)/shard_map/psum | solution.py:65
  475.5 12.4 %fusion.2 = bf16[8192,1024]{0,1:T(8,128)(2,1)} fusion(bf16[2,96,8192]{2,1,0:T(8,128)(2,1)} %all-gather.4.cloned.1.call-done, f32[2,96,1024]{2,1,0:T(8,128)S(1)} %get-tuple-element.20, f32[1,96,1024]{2,1,0:T(8,128)S(1)} %fusion.4, f32[1,96,1024]{2,1,0:T(8,128)} %copy-done.1, f32[2,1024]{1,0:T(2,128)S(1)} %get-tuple-element.21, ...), kind=kOutput, calls=%fused_computation.3 | convolution fusion | flops 3231186944 | bytes 21528576 | tf_op jit(solution)/shard_map/dot_general | solution.py:74
  490.6 41.4 %all-reduce = (f32[]{:T(128)}, f32[]{:T(128)}) all-reduce(f32[]{:T(128)S(6)} %add.47, f32[]{:T(128)S(6)} %sub.40), channel_id=1, replica_groups=mesh['dp'=4,'feat'=8] {'dp','feat'}, use_global_device_ids=true, to_apply=%region_9.10 | all-reduce | flops 2 | bytes 16 | tf_op jit(solution)/shard_map/psum | solution.py:51
  533.3 0.7 bitcast_select_fusion
  534.0 232.7 %reduce-scatter.2.cloned.1.call-done = bf16[2048,1024]{0,1:T(8,128)(2,1)} async-done(((bf16[8192,1024]{0,1:T(8,128)(2,1)}), bf16[2048,1024]{0,1:T(8,128)(2,1)}) %reduce-scatter.2.cloned.1.call-update) | async-done | bytes 4194320 | tf_op jit(solution)/shard_map/reduce_scatter | solution.py:73
  766.7 6.6 convert_multiply_fusion
  773.4 9.2 %copy.6 = f32[2048,1024]{1,0:T(8,128)} copy(f32[2048,1024]{0,1:T(8,128)} %convert_multiply_fusion) | data formatting | bytes 16777216
  (21 shorter events, 1.3 us)
Async XLA Ops:
  7.2 37.8 %all-gather.4.cloned.1.call-start = ((), (), s32[]{:S(2)}) async-start(), calls=%async_computation.1 | async-start | bytes 3538944 | tf_op jit(solution)/shard_map/all_gather | solution.py:18
  7.9 325.4 %all-gather.6.cloned.1.call-start = ((), (), s32[]{:S(2)}) async-start(), calls=%async_computation.2 | async-start | bytes 20971520 | tf_op jit(solution)/shard_map/all_gather | solution.py:22
  8.6 388.7 %all-gather.8.cloned.1.call-start = ((), (), s32[]{:S(2)}) async-start(), calls=%async_computation.3 | async-start | bytes 1966080 | tf_op jit(solution)/shard_map/all_gather | solution.py:32
  362.0 90.4 %all-reduce.4.cloned.1.call-start = ((), (), s32[]{:S(2)}) async-start(), calls=%async_computation.4 | async-start | bytes 589824 | tf_op jit(solution)/shard_map/psum | solution.py:34
  397.3 57.5 %copy-start = (bf16[2,384,1024]{2,1,0:T(8,128)(2,1)S(1)}, bf16[2,384,1024]{2,1,0:T(8,128)(2,1)}, u32[]{:S(2)}) copy-start(bf16[2,384,1024]{2,1,0:T(8,128)(2,1)} %all-gather.8.cloned.1.call-done) | copy-start | bytes 4718596
  400.3 366.4 %reduce-scatter.2.cloned.1.call-start = ((), (), s32[]{:S(2)}) async-start(), calls=%async_computation.5 | async-start | bytes 20971520 | tf_op jit(solution)/shard_map/reduce_scatter | solution.py:73
  455.8 0.7 copy-start.1
  487.9 1.4 copy-start.2
Sparse Core Ops, SparseCore 0:
  9.9 35.0 all-gather.3
  46.5 286.7 all-gather.5
  362.1 35.1 all-gather.7
  400.5 51.9 all-reduce.3
  488.0 278.6 reduce-scatter.1
where the time goes:
time: 792 us; the launch traced here: 791 us
  waiting for transfers between devices  636 us (80%)
  blocking collectives  87.9 us (11%)
  matrix products  26.2 us (3%)
  between operations  19.5 us (2%)
  other arithmetic  11.4 us (1%)
  local copies, waits for them, and re-layouts  9.99 us (1%)
    all_gather x1, waiting for transfers between devices, per_device(): lax.all_gather(proj_weight, 'dp', axis=0, tiled=True)  288 us
    reduce_scatter x1, waiting for transfers between devices, per_device(): lax.psum_scatter(jnp.dot(stacked.T, flat_grad, preferred_element_type=jnp...  233 us
    psum x1, waiting for transfers between devices, per_device(): grams = lax.psum(gram_part, 'feat')  50.8 us
    psum x1, blocking collectives, per_device(): total_loss, off_sum = lax.psum((loss_term, off_term), ('dp', 'feat'))  41.4 us
    all_gather x1, waiting for transfers between devices, per_device(): gathered = lax.all_gather(clip_feats, 'feat', axis=2, tiled=True)  36.3 us
    all_gather x1, waiting for transfers between devices, per_device(): batch_all = lax.all_gather(quantized, 'dp', axis=1, tiled=True)  26.6 us
    psum x1, blocking collectives, per_device(): lax.psum((jnp.sum(grad_norm, axis=1), jnp.sum(grad_norm * normed, axis=1)...  18.7 us
  transfers between devices with their start and end apart: 5, of which 5 were waited for; matrix products, arithmetic and copies ran while one was open for 0% of the time, Pallas kernels for 0%

commit v1 on v0

--- a/solution.py
+++ b/solution.py
@@ -31,7 +31,7 @@
     widened = quantized.astype(jnp.float32)
     batch_all = lax.all_gather(quantized, "dp", axis=1, tiled=True)
     gram_part = jnp.einsum("vpc,vnc->vpn", quantized, batch_all, preferred_element_type=jnp.float32)
-    grams = lax.psum(gram_part, "feat")
+    grams = jnp.sum(lax.all_gather(gram_part, "feat"), axis=0)
     total_pairs = grams.shape[2]
     row_ids = (
         lax.broadcasted_iota(jnp.int32, (pairs, total_pairs), 0) + lax.axis_index("dp") * pairs

time: 792 us -> 767 us (0.968)
  waiting for transfers between devices: 636 us -> 612 us
    psum x1 -> x0, waiting for transfers between devices: 50.8 us -> none  [per_device(): grams = lax.psum(gram_part, 'feat')]
    all_gather x0 -> x1, waiting for transfers between devices: none -> 17.7 us  [per_device(): grams = jnp.sum(lax.all_gather(gram_part, 'feat'), axis=0)]
    all_gather x1, waiting for transfers between devices: 26.6 us -> 35.3 us  [per_device(): batch_all = lax.all_gather(quantized, 'dp', axis=1, tiled=True)]
where the time goes in v1:
time: 767 us
  waiting for transfers between devices  612 us (80%)
  blocking collectives  88.8 us (12%)
  matrix products  24.5 us (3%)
  between operations  19.4 us (3%)
  other arithmetic  11.7 us (2%)
  local copies, waits for them, and re-layouts  10.2 us (1%)
    all_gather x1, waiting for transfers between devices, per_device(): lax.all_gather(proj_weight, 'dp', axis=0, tiled=True)  288 us
    reduce_scatter x1, waiting for transfers between devices, per_device(): lax.psum_scatter(jnp.dot(stacked.T, flat_grad, preferred_element_type=jnp...  233 us
    psum x1, blocking collectives, per_device(): total_loss, off_sum = lax.psum((loss_term, off_term), ('dp', 'feat'))  41.3 us
    all_gather x1, waiting for transfers between devices, per_device(): gathered = lax.all_gather(clip_feats, 'feat', axis=2, tiled=True)  36.3 us
    all_gather x1, waiting for transfers between devices, per_device(): batch_all = lax.all_gather(quantized, 'dp', axis=1, tiled=True)  35.3 us
    psum x1, blocking collectives, per_device(): lax.psum((jnp.sum(grad_norm, axis=1), jnp.sum(grad_norm * normed, axis=1)...  18.7 us
    all_gather x1, waiting for transfers between devices, per_device(): grams = jnp.sum(lax.all_gather(gram_part, 'feat'), axis=0)  17.7 us
  transfers between devices with their start and end apart: 5, of which 5 were waited for; matrix products, arithmetic and copies ran while one was open for 0% of the time, Pallas kernels for 0%

profile of v1, /device:TPU:0, one launch (start us, length us, event | category | flops | bytes accessed | tf_op | source)
XLA Modules:
  0.0 766.5 jit_solution(6437498945790818519)
XLA Ops:
  7.2 0.7 all-gather.6.cloned.1.call-update
  7.9 0.7 all-gather.8.cloned.1.call-update
  8.7 36.3 %all-gather.6.cloned.1.call-done = bf16[2,96,8192]{2,1,0:T(8,128)(2,1)} async-done(((bf16[2,96,1024]{2,1,0:T(8,128)(2,1)}), bf16[2,96,8192]{2,1,0:T(8,128)(2,1)}) %all-gather.6.cloned.1.call-update) | async-done | bytes 3145744 | tf_op jit(solution)/shard_map/all_gather | solution.py:18
  45.0 288.4 %all-gather.8.cloned.1.call-done = bf16[8192,1024]{1,0:T(8,128)(2,1)} async-done(((bf16[2048,1024]{1,0:T(8,128)(2,1)}), bf16[8192,1024]{1,0:T(8,128)(2,1)}) %all-gather.8.cloned.1.call-update) | async-done | bytes 16777232 | tf_op jit(solution)/shard_map/all_gather | solution.py:22
  333.3 8.5 %fusion.16 = (f32[2,1024]{1,0:T(2,128)S(1)}, f32[2,96,1024]{2,1,0:T(8,128)S(1)}) fusion(bf16[2,96,8192]{2,1,0:T(8,128)(2,1)} %all-gather.6.cloned.1.call-done, bf16[8192,1024]{1,0:T(8,128)(2,1)} %all-gather.8.cloned.1.call-done), kind=kOutput, calls=%fused_computation.42 | convolution fusion | flops 3221420032 | bytes 20717568 | tf_op jit(solution)/shard_map/dot_general | solution.py:20
  341.8 8.8 %psum.49 = f32[2,1024]{1,0:T(2,128)S(1)} all-reduce(f32[2,1024]{1,0:T(2,128)S(1)} %get-tuple-element.23), channel_id=1, replica_groups=mesh['dp'=4,'feat'=8] {'dp'}, use_global_device_ids=true, to_apply=%region_1.0 | all-reduce | flops 2048 | bytes 16384 | tf_op jit(solution)/shard_map/psum | solution.py:25
  350.7 10.3 %psum.50 = f32[2,1024]{1,0:T(2,128)S(1)} all-reduce(f32[2,1024]{1,0:T(2,128)S(1)} %multiply_reduce_fusion.1), channel_id=1, replica_groups=mesh['dp'=4,'feat'=8] {'dp'}, use_global_device_ids=true, to_apply=%region_3.0 | all-reduce | flops 2048 | bytes 16384 | tf_op jit(solution)/shard_map/psum | solution.py:27
  361.1 0.9 fusion.14
  362.0 35.3 %all-gather.10.cloned.1.call-done = bf16[2,384,1024]{2,1,0:T(8,128)(2,1)} async-done(((bf16[2,96,1024]{2,1,0:T(8,128)(2,1)}), bf16[2,384,1024]{2,1,0:T(8,128)(2,1)}) %all-gather.10.cloned.1.call-update) | async-done | bytes 1572880 | tf_op jit(solution)/shard_map/all_gather | solution.py:32
  397.3 3.0 fusion.17
  400.4 9.6 %psum.51 = f32[1024]{0:T(1024)S(1)} all-reduce(f32[1024]{0:T(1024)S(1)} %multiply_reduce_fusion.2), channel_id=1, replica_groups=mesh['dp'=4,'feat'=8] {'dp'}, use_global_device_ids=true, to_apply=%region_5.6 | all-reduce | flops 1024 | bytes 8192 | tf_op jit(solution)/shard_map/psum | solution.py:43
  410.1 0.6 multiply_reduce_fusion.4
  410.7 17.7 %all-gather.12.cloned.1.call-done = f32[16,96,384]{2,1,0:T(8,128)} async-done(((f32[2,96,384]{2,1,0:T(8,128)}), f32[16,96,384]{2,1,0:T(8,128)}) %all-gather.12.cloned.1.call-update) | async-done | bytes 2359312 | tf_op jit(solution)/shard_map/all_gather | solution.py:34
  428.4 1.8 reduce_sum.85
  430.8 0.4 copy-done.1
  431.5 0.5 copy-done.2
  432.0 18.7 %all-reduce.1 = (f32[2,1024]{1,0:T(2,128)S(1)}, f32[2,1024]{1,0:T(2,128)S(1)}) all-reduce(f32[2,1024]{1,0:T(2,128)S(1)} %get-tuple-element.13, f32[2,1024]{1,0:T(2,128)S(1)} %get-tuple-element.12), channel_id=1, replica_groups=mesh['dp'=4,'feat'=8] {'dp'}, use_global_device_ids=true, to_apply=%region_13.14 | all-reduce | flops 4096 | bytes 32768 | tf_op jit(solution)/shard_map/psum | solution.py:65
  450.7 12.5 %fusion.2 = bf16[8192,1024]{0,1:T(8,128)(2,1)} fusion(bf16[2,96,8192]{2,1,0:T(8,128)(2,1)} %all-gather.6.cloned.1.call-done, f32[2,96,1024]{2,1,0:T(8,128)S(1)} %get-tuple-element.24, f32[1,96,1024]{2,1,0:T(8,128)} %copy-done.1, f32[1,96,1024]{2,1,0:T(8,128)} %copy-done.2, f32[2,1024]{1,0:T(2,128)S(1)} %get-tuple-element.25, ...), kind=kOutput, calls=%fused_computation.3 | convolution fusion | flops 3231186944 | bytes 21528576 | tf_op jit(solution)/shard_map/dot_general | solution.py:74
  464.5 0.6 multiply_reduce_fusion.3
  465.8 41.3 %all-reduce = (f32[]{:T(128)}, f32[]{:T(128)}) all-reduce(f32[]{:T(128)S(6)} %add.45, f32[]{:T(128)S(6)} %sub.40), channel_id=1, replica_groups=mesh['dp'=4,'feat'=8] {'dp','feat'}, use_global_device_ids=true, to_apply=%region_9.10 | all-reduce | flops 2 | bytes 16 | tf_op jit(solution)/shard_map/psum | solution.py:51
  508.4 0.7 bitcast_select_fusion
  509.2 232.7 %reduce-scatter.2.cloned.1.call-done = bf16[2048,1024]{0,1:T(8,128)(2,1)} async-done(((bf16[8192,1024]{0,1:T(8,128)(2,1)}), bf16[2048,1024]{0,1:T(8,128)(2,1)}) %reduce-scatter.2.cloned.1.call-update) | async-done | bytes 4194320 | tf_op jit(solution)/shard_map/reduce_scatter | solution.py:73
  741.9 6.6 convert_multiply_fusion
  748.5 9.2 %copy.7 = f32[2048,1024]{1,0:T(8,128)} copy(f32[2048,1024]{0,1:T(8,128)} %convert_multiply_fusion) | data formatting | bytes 16777216
  (22 shorter events, 1.3 us)
Async XLA Ops:
  7.2 37.8 %all-gather.6.cloned.1.call-start = ((), (), s32[]{:S(2)}) async-start(), calls=%async_computation.1 | async-start | bytes 3538944 | tf_op jit(solution)/shard_map/all_gather | solution.py:18
  7.9 325.4 %all-gather.8.cloned.1.call-start = ((), (), s32[]{:S(2)}) async-start(), calls=%async_computation.2 | async-start | bytes 20971520 | tf_op jit(solution)/shard_map/all_gather | solution.py:22
  8.6 388.7 %all-gather.10.cloned.1.call-start = ((), (), s32[]{:S(2)}) async-start(), calls=%async_computation.3 | async-start | bytes 1966080 | tf_op jit(solution)/shard_map/all_gather | solution.py:32
  362.0 66.4 %all-gather.12.cloned.1.call-start = ((), (), s32[]{:S(2)}) async-start(), calls=%async_computation.5 | async-start | bytes 2654208 | tf_op jit(solution)/shard_map/all_gather | solution.py:34
  397.3 32.9 %copy-start = (bf16[2,384,1024]{2,1,0:T(8,128)(2,1)S(1)}, bf16[2,384,1024]{2,1,0:T(8,128)(2,1)}, u32[]{:S(2)}) copy-start(bf16[2,384,1024]{2,1,0:T(8,128)(2,1)} %all-gather.10.cloned.1.call-done) | copy-start | bytes 4718596
  400.3 341.6 %reduce-scatter.2.cloned.1.call-start = ((), (), s32[]{:S(2)}) async-start(), calls=%async_computation.4 | async-start | bytes 20971520 | tf_op jit(solution)/shard_map/reduce_scatter | solution.py:73
  430.5 0.7 copy-start.1
  431.3 0.7 copy-start.2
Sparse Core Ops, SparseCore 0:
  9.9 35.0 all-gather.5
  46.5 286.7 all-gather.7
  362.1 35.1 all-gather.9
  400.4 27.8 all-gather.11
  463.3 278.4 reduce-scatter.1
